TPU v7x, 1024 devices: a whole 8x8x8 slice. The times are simulated.
1024 devices in a mesh: expert: 64 (over z, x), tensor: 16 (over y, core).
Axes of the slice: x: 8, y: 8, z: 8, core: 2. Of those that a mesh axis runs over, the one named last changes fastest.
Arguments:
- hidden: bfloat16 [64, 1536, 2048], P('expert'), may hold values from -6 to 6
- down_weight: bfloat16 [64, 2048, 7168], P('expert', None, 'tensor'), may hold values from -0.125 to 0.125
- expert_ids: int32 [8192, 8], P('expert'), may hold values from 0 to 63, as said below
- gate_weights: float32 [8192, 8], P('expert'), may hold values from 0.1 to 0.6
- residual: bfloat16 [8192, 7168], P('expert', 'tensor'), may hold values from -36 to 36
- norm_gain: float32 [7168], replicated, may hold values from 0.1 to 1.9
- proj_weight: bfloat16 [7168, 2112], P(None, 'tensor'), may hold values from -0.0625 to 0.0625
Outputs:
- stream: bfloat16 [8192, 7168], P('expert', 'tensor')
- latents: bfloat16 [8192, 2112], P('expert', 'tensor')
Inputs may be any that keep to these rules, and one draw needn't show every extreme that they name: `expert_ids`: experts 4 g to 4 g + 3 form node group g. Each token names 8 different experts, two in each of exactly 4 node groups. Within each aligned block of 128 tokens no expert is named by more than 24 tokens and no node group is used by more than 48 tokens; in every block some node group is used by exactly 48 tokens and each of its experts is named by exactly 24.
All inputs are finite; a program needn't handle non-finite values.
Results may differ from a plain program's by a relative error of at most 0.014.
Values may be sent and summed in bfloat16 or wider, within the bound.
A program may use at most 64 MiB of HBM per device.

v0:
```python
import jax
import jax.numpy as jnp
from jax import lax
from jax.sharding import PartitionSpec as P

D = 7168
NODE_SIZE = 4


epsilon = 1e-06


def joined_along(tiles, dim):
    shape = list(tiles.shape[1:])
    shape[dim] *= tiles.shape[0]
    return jnp.moveaxis(tiles, 0, dim).reshape(shape)


def sent_to_all(array, axis):
    copies = jnp.broadcast_to(array, (lax.axis_size(axis), *array.shape))
    return lax.all_to_all(copies, axis, split_axis=0, concat_axis=0, tiled=True)


def gather_directly(array, axis, dim):
    return joined_along(sent_to_all(array, axis), dim)


def on_device(hidden, down_weight, expert_ids, gate_weights, residual, norm_gain, proj_weight):
    devices = lax.axis_size("expert")
    local_experts = hidden.shape[0]
    capacity = hidden.shape[1] // devices
    columns = down_weight.shape[2]
    experts = local_experts * devices
    group_count = experts // NODE_SIZE
    outputs = jnp.einsum(
        "xsf,xfd->xsd", hidden, down_weight, preferred_element_type=jnp.float32
    ).astype(jnp.bfloat16)
    grouped = outputs.reshape(local_experts, devices, capacity, columns)
    returned = lax.all_to_all(grouped, "expert", split_axis=1, concat_axis=0, tiled=True)
    returned = returned.reshape(experts * capacity, columns)
    expert_range = jnp.arange(experts, dtype=jnp.int32)
    counts = jnp.sum((expert_ids[:, :, None] == expert_range).astype(jnp.int32), axis=1)
    before = jnp.cumsum(counts, axis=0) - counts
    slot_index = jnp.take_along_axis(before, expert_ids, axis=1)
    flat_rows = expert_ids * capacity + slot_index
    picked = returned[flat_rows]
    gated = gate_weights[:, :, None] * picked.astype(jnp.float32)
    membership = (
        expert_ids[:, :, None] // NODE_SIZE == jnp.arange(group_count, dtype=jnp.int32)
    ).astype(jnp.float32)
    group_sums = jnp.einsum("tkg,tkd->tgd", membership, gated)
    group_parts = lax.optimization_barrier(group_sums.astype(jnp.bfloat16))
    summed = residual.astype(jnp.float32) + jnp.sum(group_parts.astype(jnp.float32), axis=1)
    stream = summed.astype(jnp.bfloat16)
    section_wide = gather_directly(stream, "tensor", 1).astype(jnp.float32)
    normed_part = (section_wide * norm_gain).astype(jnp.bfloat16)
    added = jnp.dot(normed_part, proj_weight, preferred_element_type=jnp.float32)
    energy = jnp.sum(section_wide * section_wide, axis=1)
    inverse = lax.rsqrt(energy / D + epsilon)
    latents = (added * inverse[:, None]).astype(jnp.bfloat16)
    return (stream, latents)


def solution(mesh):
    return jax.shard_map(
        on_device,
        mesh=mesh,
        in_specs=(
            P("expert", None, None),
            P("expert", None, "tensor"),
            P("expert", None),
            P("expert", None),
            P("expert", "tensor"),
            P(),
            P(None, "tensor"),
        ),
        out_specs=(P("expert", "tensor"), P("expert", "tensor")),
        check_vma=False,
    )
```

profile of v0, /device:TPU:1, one launch (start us, length us, event | category | flops | bytes accessed | tf_op | source)
XLA Modules:
  0.0 140.7 jit_solution(10454975125300735057)
XLA Ops:
  0.6 0.0 copy-start
  0.6 6.5 %fusion.3 = bf16[1536,448]{0,1:T(8,128)(2,1)S(1)} fusion(bf16[1,1536,2048]{2,1,0:T(8,128)(2,1)} %param.7, bf16[1,2048,448]{1,2,0:T(8,128)(2,1)} %param.8), kind=kOutput, calls=%fused_computation.8 | convolution fusion | flops 2819260416 | bytes 9502720 | tf_op jit(solution)/shard_map/xsf,xfd->xsd/dot_general | solution.py:35
  7.1 1.6 %copy.62 = bf16[1536,448]{1,0:T(8,128)(2,1)} copy(bf16[1536,448]{0,1:T(8,128)(2,1)S(1)} %fusion.3) | data formatting | bytes 2752512 | tf_op jit(solution)/shard_map/convert_element_type | solution.py:37
  8.7 0.0 copy-start.3
  8.7 23.5 %all-to-all-start = ((bf16[1,64,24,448]{3,2,0,1:T(8,128)(2,1)}), bf16[1,64,24,448]{3,2,0,1:T(8,128)(2,1)}, u32[]{:S(2)}, u32[]{:S(2)}) async-start(bf16[1,64,24,448]{3,2,0,1:T(8,128)(2,1)} %bitcast.3), calls=%async_computation | async-start | bytes 3145728 | tf_op jit(solution)/shard_map/all_to_all | solution.py:39
  32.2 0.0 copy-done.3
  32.3 0.1 copy.64
  32.4 0.1 copy.66
  32.5 0.1 reshape.76
  32.6 0.2 reduce_window_sum.11
  32.8 0.0 copy-start.5
  32.8 0.0 copy-start.2
  32.8 7.1 %gather_fusion.1 = s32[1024]{0:T(1024)S(1)} fusion(s32[128,64]{1,0:T(8,128)S(1)} %sub.10, s32[1024]{0:T(1024)S(1)} %reshape.76), kind=kCustom, calls=%fused_computation.1 | custom fusion | bytes 16384 | tf_op jit(solution)/shard_map/jit(take_along_axis)/gather | solution.py:44
  39.9 0.1 reshape.79
  40.1 0.1 copy.60
  40.2 0.1 copy.68
  40.3 0.1 reshape.70
  40.4 0.0 copy-done.5
  40.4 0.1 copy.61
  40.5 0.0 copy-done.2
  40.5 0.1 copy.59
  40.6 30.6 %all-to-all-done = bf16[1,64,24,448]{3,2,0,1:T(8,128)(2,1)} async-done(((bf16[1,64,24,448]{3,2,0,1:T(8,128)(2,1)}), bf16[1,64,24,448]{3,2,0,1:T(8,128)(2,1)}, u32[]{:S(2)}, u32[]{:S(2)}) %all-to-all-start) | async-done | bytes 1376288 | tf_op jit(solution)/shard_map/all_to_all | solution.py:39
  71.2 5.6 %gather_fusion = bf16[1024,448]{1,0:T(8,128)(2,1)S(1)} fusion(bf16[1536,448]{1,0:T(8,128)(2,1)} %bitcast.4, s32[1024]{0:T(1024)S(1)} %broadcast_clamp_fusion), kind=kCustom, calls=%fused_computation | custom fusion | bytes 1839104 | tf_op jit(solution)/shard_map/gather | solution.py:46
  76.8 1.3 fusion.7
  78.1 0.9 convert_reduce_fusion
  79.0 0.1 copy.70
  79.2 0.0 copy-start.1
  79.2 0.3 broadcast_in_dim.10
  79.5 0.0 copy-start.4
  79.6 55.9 %all_to_all.14 = bf16[16,128,448]{1,2,0:T(8,128)(2,1)S(1)} all-to-all(bf16[16,128,448]{1,2,0:T(8,128)(2,1)S(1)} %broadcast_in_dim.10), channel_id=1, replica_groups=mesh['expert'=64,'tensor'=16] {'tensor'}, dimensions={0} | all-to-all | bytes 3670016 | tf_op jit(solution)/shard_map/all_to_all | solution.py:21
  135.4 0.0 copy-done.1
  135.4 1.0 multiply_reduce_fusion
  136.4 0.0 copy-done.4
  136.4 3.0 %fusion.2 = bf16[128,7168]{0,1:T(8,128)(2,1)S(1)} fusion(f32[7168]{0:T(1024)S(1)} %copy-done.4, bf16[16,128,448]{1,2,0:T(8,128)(2,1)S(1)} %all_to_all.14), kind=kLoop, calls=%fused_computation.6 | loop fusion | flops 2752512 | bytes 3698688 | tf_op jit(solution)/shard_map/convert_element_type | solution.py:56
  139.4 0.0 copy-done
  139.4 1.3 fusion.9
  (8 shorter events, 0.2 us)
Async XLA Ops:
  0.6 138.8 %copy-start = (bf16[7168,132]{0,1:T(8,128)(2,1)S(1)}, bf16[7168,132]{0,1:T(8,128)(2,1)}, u32[]{:S(2)}) copy-start(bf16[7168,132]{0,1:T(8,128)(2,1)} %param.13) | copy-start | bytes 5677060
  8.7 23.5 %copy-start.3 = (s32[128,8]{0,1:T(8,128)S(1)}, s32[128,8]{0,1:T(8,128)}, u32[]{:S(2)}) copy-start(s32[128,8]{0,1:T(8,128)} %param.9) | copy-start | bytes 12292
  8.7 62.5 %all-to-all-start = ((bf16[1,64,24,448]{3,2,0,1:T(8,128)(2,1)}), bf16[1,64,24,448]{3,2,0,1:T(8,128)(2,1)}, u32[]{:S(2)}, u32[]{:S(2)}) async-start(bf16[1,64,24,448]{3,2,0,1:T(8,128)(2,1)} %bitcast.3), calls=%async_computation | async-start | bytes 3145728 | tf_op jit(solution)/shard_map/all_to_all | solution.py:39
  32.8 7.6 %copy-start.5 = (f32[128,8]{0,1:T(8,128)S(1)}, f32[128,8]{0,1:T(8,128)}, u32[]{:S(2)}) copy-start(f32[128,8]{0,1:T(8,128)} %param.10) | copy-start | bytes 12292
  32.8 7.7 %copy-start.2 = (bf16[128,448]{0,1:T(8,128)(2,1)S(1)}, bf16[128,448]{0,1:T(8,128)(2,1)}, u32[]{:S(2)}) copy-start(bf16[128,448]{0,1:T(8,128)(2,1)} %param.11) | copy-start | bytes 344068
  79.2 56.2 %copy-start.1 = (bf16[128,448]{0,1:T(8,128)(2,1)}, bf16[128,448]{0,1:T(8,128)(2,1)S(1)}, u32[]{:S(2)}) copy-start(bf16[128,448]{0,1:T(8,128)(2,1)S(1)} %copy.70) | copy-start | bytes 344068
  79.5 56.8 %copy-start.4 = (f32[7168]{0:T(1024)S(1)}, f32[7168]{0:T(1024)}, u32[]{:S(2)}) copy-start(f32[7168]{0:T(1024)} %param.12) | copy-start | bytes 86020
where the time goes:
time: 141 us
  blocking collectives  55.9 us (40%)
  waiting for transfers between devices  30.6 us (22%)
  starting transfers between devices  23.5 us (17%)
  local copies, waits for them, and re-layouts  15.7 us (11%)
  matrix products  9.08 us (6%)
  other arithmetic  5.18 us (4%)
    all_to_all x1, blocking collectives, sent_to_all(): return lax.all_to_all(copies, axis, split_axis=0, concat_axis=0, tiled=True)  55.9 us
    all_to_all x1, waiting for transfers between devices, on_device(): lax.all_to_all(grouped, 'expert', split_axis=1, concat_axis=0, tiled=True)  30.6 us
    all_to_all x1, starting transfers between devices, on_device(): lax.all_to_all(grouped, 'expert', split_axis=1, concat_axis=0, tiled=True)  23.5 us
    gather x5, local copies, waits for them, and re-layouts, on_device(): slot_index = jnp.take_along_axis(before, expert_ids, axis=1)  7.39 us
    dot_general x1, matrix products, on_device(): jnp.einsum('xsf,xfd->xsd', hidden, down_weight, preferred_element_type=jn...  6.49 us
    gather x1, local copies, waits for them, and re-layouts, on_device(): picked = returned[flat_rows]  5.6 us
    convert_element_type x1, other arithmetic, on_device(): normed_part = (section_wide * norm_gain).astype(jnp.bfloat16)  3 us
  transfers between devices with their start and end apart: 1, of which 1 were waited for; matrix products, arithmetic and copies ran while one was open for 6% of the time, Pallas kernels for 0%

commit v1 on v0

v1 whole, which is shorter than its diff:
```python
import jax
import jax.numpy as jnp
from jax import lax
from jax.experimental import pallas as pl
from jax.experimental.pallas import tpu as pltpu
from jax.sharding import PartitionSpec as P

MESH = pl.DeviceIdType.MESH
F32 = jnp.float32
BF16 = jnp.bfloat16

D = 7168
SIDE = 8
CAP = 24
TOKENS = 128
ROWS = SIDE * CAP
PAIR = 2 * CAP
COLS = 448
LATENT = 132
HOPS = (1, 7, 2, 6, 3, 5, 4)
X_FIRST = (True, False, True, False)
epsilon = 1e-06


def kernel(
    hidden_ref, down_ref, proj_ref, meta_ref, residual_ref, gain_ref,
    stream_ref, latents_ref,
    hid, wts, wts2, proj, meta_x, meta_z, gate_x, gate_z,
    out, out3, got, got3, part, part3, came, came3, all_, all3, acc, square,
    load_sem, hid_sem, meta_ss, meta_rs, one_ss, one_rs, two_ss, two_rs, ring_ss, ring_rs,
):
    expert = lax.axis_index("expert")
    tensor = lax.axis_index("tensor")
    z, x = expert // SIDE, expert % SIDE
    y, core = tensor // 2, tensor % 2
    lane = lax.broadcasted_iota(jnp.int32, (1, 128), 1)
    low = lane < 64

    load_w = pltpu.make_async_copy(down_ref, wts, load_sem.at[0])
    load_w.start()

    def load_hidden(tile):
        rows = pl.ds(pl.multiple_of(tile * 2 * ROWS, 2 * ROWS), 2 * ROWS)
        return pltpu.make_async_copy(hidden_ref.at[rows], hid.at[rows], hid_sem.at[tile])

    for tile in range(4):
        load_hidden(tile).start()
    load_p = pltpu.make_async_copy(proj_ref, proj, load_sem.at[1])
    load_p.start()

    def along_x(index):
        return {"expert": z * SIDE + index, "tensor": tensor}

    def along_z(index):
        return {"expert": index * SIDE + x, "tensor": tensor}

    def along_y(index):
        return {"expert": expert, "tensor": index * 2 + core}

    partner = {"expert": expert, "tensor": y * 2 + 1 - core}
    up, down = (y + 1) % SIDE, (y + SIDE - 1) % SIDE

    barrier = pltpu.get_barrier_semaphore()
    for hop in HOPS:
        pl.semaphore_signal(barrier, inc=1, device_id=along_x((x + hop) % SIDE), device_id_type=MESH)
        pl.semaphore_signal(barrier, inc=1, device_id=along_z((z + hop) % SIDE), device_id_type=MESH)
    pl.semaphore_signal(barrier, inc=1, device_id=along_y(up), device_id_type=MESH)
    pl.semaphore_signal(barrier, inc=1, device_id=along_y(down), device_id_type=MESH)
    pl.semaphore_signal(barrier, inc=1, device_id=partner, device_id_type=MESH)
    pl.semaphore_wait(barrier, 17)

    def remote(source, target, send_sem, recv_sem, device):
        return pltpu.make_async_remote_copy(
            src_ref=source, dst_ref=target, send_sem=send_sem, recv_sem=recv_sem,
            device_id=device, device_id_type=MESH,
        )

    def meta_copies(hop):
        to_z, to_x = (z + hop) % SIDE, (x + hop) % SIDE
        return (
            remote(meta_ref, meta_x.at[z], meta_ss.at[0, hop], meta_rs.at[0, z], along_z(to_z)),
            remote(meta_ref, meta_z.at[x], meta_ss.at[1, hop], meta_rs.at[1, x], along_x(to_x)),
        )

    for hop in HOPS:
        for copy in meta_copies(hop):
            copy.start()
    meta_x[z] = meta_ref[...]
    meta_z[x] = meta_ref[...]

    def buffers(chunk):
        if chunk < 3:
            return out.at[chunk], got.at[chunk], part.at[chunk], came.at[chunk], all_.at[chunk]
        return out3, got3, part3, came3, all3

    def first_axis(chunk):
        return (x, along_x) if X_FIRST[chunk] else (z, along_z)

    def second_axis(chunk):
        return (z, along_z) if X_FIRST[chunk] else (x, along_x)

    def one_copy(chunk, hop):
        source, target = buffers(chunk)[:2]
        me, along = first_axis(chunk)
        to = (me + hop) % SIDE
        return remote(source.at[to], target.at[me], one_ss.at[chunk, hop], one_rs.at[chunk, me], along(to))

    def one_arrival(chunk, hop):
        source, target = buffers(chunk)[:2]
        me, along = first_axis(chunk)
        origin = (me + hop) % SIDE
        return remote(source.at[me], target.at[origin], one_ss.at[chunk, hop], one_rs.at[chunk, origin], along(origin))

    def two_copy(chunk, hop):
        source, target = buffers(chunk)[2:4]
        me, along = second_axis(chunk)
        to = (me + hop) % SIDE
        return remote(source.at[to], target.at[me], two_ss.at[chunk, hop], two_rs.at[chunk, me], along(to))

    def two_arrival(chunk, hop):
        source, target = buffers(chunk)[2:4]
        me, along = second_axis(chunk)
        origin = (me + hop) % SIDE
        return remote(source.at[me], target.at[origin], two_ss.at[chunk, hop], two_rs.at[chunk, origin], along(origin))

    def keep_own(chunk):
        source, target = buffers(chunk)[:2]
        me, _ = first_axis(chunk)
        target[me] = source[me]

    def tile_rows(tile):
        return pl.ds(pl.multiple_of(tile * 2 * ROWS, 2 * ROWS), 2 * ROWS)

    def store_x_first(chunk, tile, value):
        rows = pl.ds(pl.multiple_of(tile * PAIR, 16), PAIR)
        for j in range(SIDE):
            both = jnp.concatenate(
                [value[j * CAP:(j + 1) * CAP], value[ROWS + j * CAP:ROWS + (j + 1) * CAP]], axis=0
            )
            out[chunk, j, rows, :] = both.astype(BF16)

    load_w.wait()

    def first_half(tile, carry):
        load_hidden(tile).wait()
        value = jnp.dot(hid[tile_rows(tile), :], wts[:, 0:256], preferred_element_type=F32)
        store_x_first(0, tile, value[:, :128])
        for q in range(2):
            out[1, 2 * tile + q] = value[q * ROWS:(q + 1) * ROWS, 128:].astype(BF16)
        return carry

    lax.fori_loop(0, 4, first_half, 0)
    for hop in HOPS:
        one_copy(0, hop).start()
        one_copy(1, hop).start()
    keep_own(0)
    keep_own(1)

    wts2[:, :128] = wts[:, 256:384]
    last = wts[:, 384:448]
    wts2[:, 128:] = jnp.concatenate([last, last], axis=1)

    def second_half(tile, carry):
        value = jnp.dot(hid[tile_rows(tile), :], wts2[...], preferred_element_type=F32)
        store_x_first(2, tile, value[:, :128])
        for q in range(2):
            wide = value[q * ROWS:(q + 1) * ROWS, 128:]
            out3[2 * tile + q] = jnp.where(low, wide[:ROWS // 2], wide[ROWS // 2:]).astype(BF16)
        return carry

    lax.fori_loop(0, 4, second_half, 0)
    for hop in HOPS:
        one_copy(2, hop).start()
        one_copy(3, hop).start()
    keep_own(2)
    keep_own(3)

    for hop in HOPS:
        to_z, to_x = (z + hop) % SIDE, (x + hop) % SIDE
        remote(meta_ref, meta_x.at[to_z], meta_ss.at[0, hop], meta_rs.at[0, to_z], along_z(to_z)).wait_recv()
        remote(meta_ref, meta_z.at[to_x], meta_ss.at[1, hop], meta_rs.at[1, to_x], along_x(to_x)).wait_recv()
    earlier = (
        lax.broadcasted_iota(jnp.int32, (128, 128), 0) < lax.broadcasted_iota(jnp.int32, (128, 128), 1)
    ).astype(BF16)
    place = lax.broadcasted_iota(jnp.int32, (CAP, 128), 0).astype(F32)
    nothing = jnp.zeros((CAP, 128), F32)

    def build(meta, gates, base, step):
        def pair(p, carry):
            blocks = []
            for q in range(2):
                info = meta[2 * p + q]
                ids, weights = info[:8], info[8:]
                used, gate = [], []
                for a in range(SIDE):
                    match = ids == (base + a * step).astype(F32)
                    used.append(jnp.sum(jnp.where(match, 1.0, 0.0), axis=0, keepdims=True))
                    gate.append(jnp.sum(jnp.where(match, weights, 0.0), axis=0, keepdims=True))
                chosen = jnp.concatenate(used, axis=0)
                before = jnp.dot(chosen.astype(BF16), earlier, preferred_element_type=F32)
                where = jnp.where(chosen > 0.5, before, -1.0)
                blocks.append([jnp.where(where[a:a + 1] == place, gate[a], 0.0) for a in range(SIDE)])
            rows = []
            for a in range(SIDE):
                rows.append(jnp.concatenate([blocks[0][a], nothing], axis=1))
                rows.append(jnp.concatenate([nothing, blocks[1][a]], axis=1))
            gates[p] = jnp.concatenate(rows, axis=0).T.astype(BF16)
            return carry

        lax.fori_loop(0, 4, pair, 0)

    build(meta_x, gate_x, z * SIDE, jnp.int32(1))
    build(meta_z, gate_z, x, jnp.int32(SIDE))

    def merge(chunk):
        for hop in HOPS:
            one_arrival(chunk, hop).wait_recv()
        gates = gate_x if X_FIRST[chunk] else gate_z

        def pair(p, carry):
            rows = pl.ds(pl.multiple_of(p * PAIR, 16), PAIR)
            met = jnp.concatenate([got[chunk, a, rows, :] for a in range(SIDE)], axis=0)
            both = jnp.dot(gates[p], met, preferred_element_type=F32).astype(BF16)
            part[chunk, 2 * p] = both[:TOKENS]
            part[chunk, 2 * p + 1] = both[TOKENS:]
            return carry

        lax.fori_loop(0, 4, pair, 0)
        for hop in HOPS:
            two_copy(chunk, hop).start()

    def merge_last():
        for hop in HOPS:
            one_arrival(3, hop).wait_recv()
        for p in range(2):
            met = jnp.concatenate([got3[a, p * PAIR:(p + 1) * PAIR, :] for a in range(SIDE)], axis=0)
            left = jnp.dot(gate_z[p], met, preferred_element_type=F32)
            right = jnp.dot(gate_z[p + 2], met, preferred_element_type=F32)
            for q in range(2):
                value = left[q * TOKENS:(q + 1) * TOKENS]
                part3[2 * p + q] = jnp.where(low, value[:64], pltpu.roll(value[64:], 64, 1)).astype(BF16)
                value = right[q * TOKENS:(q + 1) * TOKENS]
                part3[2 * p + 4 + q] = jnp.where(low, pltpu.roll(value[:64], 64, 1), value[64:]).astype(BF16)
        for hop in HOPS:
            two_copy(3, hop).start()

    def ring_copy(chunk, source_y, device, number):
        block = buffers(chunk)[4].at[source_y * 2 + core]
        return remote(block, block, ring_ss.at[chunk, number], ring_rs.at[chunk, source_y * 2 + core], device)

    def send_own(chunk):
        ring_copy(chunk, y, along_y(up), 0).start()
        ring_copy(chunk, y, along_y(down), 1).start()
        ring_copy(chunk, y, partner, 2).start()

    def finish(chunk):
        for hop in HOPS:
            two_arrival(chunk, hop).wait_recv()
        me, _ = second_axis(chunk)
        total = residual_ref[:, chunk * 128:(chunk + 1) * 128].astype(F32) + part[chunk, me].astype(F32)
        for hop in HOPS:
            total += came[chunk, (me + hop) % SIDE].astype(F32)
        value = total.astype(BF16)
        stream_ref[:, chunk * 128:(chunk + 1) * 128] = value
        all_[chunk, tensor] = value
        send_own(chunk)

    def finish_last():
        for hop in HOPS:
            two_arrival(3, hop).wait_recv()
        me, _ = second_axis(3)
        kept = residual_ref[:, 384:448].astype(F32)
        total = jnp.concatenate([kept[:64], kept[64:]], axis=1) + part3[me].astype(F32)
        for hop in HOPS:
            total += came3[(me + hop) % SIDE].astype(F32)
        value = total.astype(BF16)
        all3[tensor] = value
        send_own(3)
        wide = value.astype(F32)
        stream_ref[0:64, 384:448] = wide[:, :64].astype(BF16)
        stream_ref[64:128, 384:448] = pltpu.roll(wide, 64, 1)[:, :64].astype(BF16)

    def from_below(chunk, step):
        return (y + SIDE - step) % SIDE

    def from_above(chunk, step):
        return (y + step) % SIDE

    def forward(chunk, step):
        origin = from_below(chunk, step)
        ring_copy(chunk, origin, along_y(up), 0).wait_recv()
        if step < 4:
            ring_copy(chunk, origin, along_y(up), 2 + step).start()
        ring_copy(chunk, origin, partner, 7 + step).start()
        if step < 4:
            origin = from_above(chunk, step)
            ring_copy(chunk, origin, along_y(down), 1).wait_recv()
            if step < 3:
                ring_copy(chunk, origin, along_y(down), 5 + step).start()
            ring_copy(chunk, origin, partner, 11 + step).start()

    def wait_partner(chunk):
        for source in range(SIDE):
            block = buffers(chunk)[4].at[source * 2 + 1 - core]
            remote(block, block, ring_ss.at[chunk, 0], ring_rs.at[chunk, source * 2 + 1 - core], partner).wait_recv()

    def project(chunk):
        wait_partner(chunk)

        def chips(source, carry):
            normed, weights = [], []
            for half in range(2):
                owner = source * 2 + half
                value = all_[chunk, owner].astype(F32)
                square[...] += value * value
                normed.append((value * gain_ref[pl.ds(owner * 4 + chunk, 1), :]).astype(BF16))
                weights.append(proj[pl.ds(pl.multiple_of(owner * COLS + chunk * 128, 16), 128), :])
            acc[...] += jnp.dot(
                jnp.concatenate(normed, axis=1), jnp.concatenate(weights, axis=0), preferred_element_type=F32
            )
            return carry

        lax.fori_loop(0, SIDE, chips, 0)

    def project_last():
        wait_partner(3)

        def chips(source, energy):
            normed, weights = [], []
            for half in range(2):
                owner = source * 2 + half
                value = all3[owner].astype(F32)
                energy = energy + value * value
                scaled = value * gain_ref[pl.ds(owner * 4 + 3, 1), :]
                normed.append(
                    jnp.concatenate([jnp.where(low, scaled, 0.0), jnp.where(low, 0.0, scaled)], axis=0).astype(BF16)
                )
                rows = proj[pl.ds(pl.multiple_of(owner * COLS + 384, 16), 64), :]
                weights += [rows, rows]
            acc[...] += jnp.dot(
                jnp.concatenate(normed, axis=1), jnp.concatenate(weights, axis=0), preferred_element_type=F32
            )
            return energy

        return lax.fori_loop(0, SIDE, chips, jnp.zeros((64, 128), F32))

    acc[...] = jnp.zeros_like(acc)
    square[...] = jnp.zeros_like(square)
    merge(0)
    merge(1)
    merge_last()
    merge(2)
    finish(0)
    load_p.wait()
    for step in range(1, 5):
        forward(0, step)
    finish(1)
    finish(2)
    finish_last()
    for step in range(1, 5):
        for chunk in (1, 2, 3):
            forward(chunk, step)
    for chunk in range(3):
        project(chunk)
    energy3 = project_last()
    energy = jnp.sum(square[...], axis=1, keepdims=True)
    energy += jnp.concatenate(
        [
            jnp.sum(jnp.where(low, energy3, 0.0), axis=1, keepdims=True),
            jnp.sum(jnp.where(low, 0.0, energy3), axis=1, keepdims=True),
        ],
        axis=0,
    )
    latents_ref[...] = (acc[...] * lax.rsqrt(energy / D + epsilon)).astype(BF16)

    for hop in HOPS:
        for copy in meta_copies(hop):
            copy.wait_send()
        for chunk in range(4):
            one_copy(chunk, hop).wait_send()
            two_copy(chunk, hop).wait_send()
    for chunk in range(4):
        for number in (0, 1, 2):
            ring_copy(chunk, y, (along_y(up), along_y(down), partner)[number], number).wait_send()
        for step in range(1, 5):
            origin = from_below(chunk, step)
            if step < 4:
                ring_copy(chunk, origin, along_y(up), 2 + step).wait_send()
            ring_copy(chunk, origin, partner, 7 + step).wait_send()
            if step < 4:
                origin = from_above(chunk, step)
                if step < 3:
                    ring_copy(chunk, origin, along_y(down), 5 + step).wait_send()
                ring_copy(chunk, origin, partner, 11 + step).wait_send()


def on_device(hidden, down_weight, expert_ids, gate_weights, residual, norm_gain, proj_weight):
    meta = jnp.concatenate([expert_ids.astype(F32), gate_weights], axis=1).T
    gain = norm_gain.reshape(16, COLS)
    gain = jnp.concatenate([gain, gain[:, 384:]], axis=1).reshape(64, 128)
    vmem = pl.BlockSpec(memory_space=pltpu.VMEM)
    hbm = pl.BlockSpec(memory_space=pl.ANY)
    dma = pltpu.SemaphoreType.DMA
    wide = (3, SIDE, ROWS, 128)
    return pl.pallas_call(
        kernel,
        name="combine",
        out_shape=(
            jax.ShapeDtypeStruct((TOKENS, COLS), BF16),
            jax.ShapeDtypeStruct((TOKENS, LATENT), BF16),
        ),
        in_specs=[hbm, hbm, hbm, vmem, vmem, vmem],
        out_specs=(vmem, vmem),
        scratch_shapes=[
            pltpu.VMEM((SIDE * ROWS, 2048), BF16),
            pltpu.VMEM((2048, COLS), BF16),
            pltpu.VMEM((2048, 256), BF16),
            pltpu.VMEM((D, LATENT), BF16),
            pltpu.VMEM((SIDE, 16, 128), F32),
            pltpu.VMEM((SIDE, 16, 128), F32),
            pltpu.VMEM((4, 2 * TOKENS, 2 * ROWS), BF16),
            pltpu.VMEM((4, 2 * TOKENS, 2 * ROWS), BF16),
            pltpu.VMEM(wide, BF16),
            pltpu.VMEM((SIDE, ROWS // 2, 128), BF16),
            pltpu.VMEM(wide, BF16),
            pltpu.VMEM((SIDE, ROWS // 2, 128), BF16),
            pltpu.VMEM((3, SIDE, TOKENS, 128), BF16),
            pltpu.VMEM((SIDE, TOKENS // 2, 128), BF16),
            pltpu.VMEM((3, SIDE, TOKENS, 128), BF16),
            pltpu.VMEM((SIDE, TOKENS // 2, 128), BF16),
            pltpu.VMEM((3, 2 * SIDE, TOKENS, 128), BF16),
            pltpu.VMEM((2 * SIDE, TOKENS // 2, 128), BF16),
            pltpu.VMEM((TOKENS, LATENT), F32),
            pltpu.VMEM((TOKENS, 128), F32),
            dma((2,)),
            dma((4,)),
            dma((2, SIDE)),
            dma((2, SIDE)),
            dma((4, SIDE)),
            dma((4, SIDE)),
            dma((4, SIDE)),
            dma((4, SIDE)),
            dma((4, 16)),
            dma((4, 16)),
        ],
        compiler_params=pltpu.CompilerParams(
            collective_id=0, has_side_effects=True, vmem_limit_bytes=56 * 1024 * 1024
        ),
    )(hidden[0], down_weight[0], proj_weight, meta, residual, gain)


def solution(mesh):
    return jax.shard_map(
        on_device,
        mesh=mesh,
        in_specs=(
            P("expert", None, None),
            P("expert", None, "tensor"),
            P("expert", None),
            P("expert", None),
            P("expert", "tensor"),
            P(),
            P(None, "tensor"),
        ),
        out_specs=(P("expert", "tensor"), P("expert", "tensor")),
        check_vma=False,
    )
```

time: 141 us -> 98.8 us (0.70)
  Pallas kernels: 0 us -> 82.1 us
  blocking collectives: 55.9 us -> 0 us
  waiting for transfers between devices: 30.6 us -> 0 us
  starting transfers between devices: 23.5 us -> 0 us
  matrix products: 9.08 us -> 0 us
  other arithmetic: 5.18 us -> 2.05 us
  local copies, waits for them, and re-layouts: 15.7 us -> 13.2 us
    pallas_call x0 -> x1, Pallas kernels: none -> 82.1 us  [on_device(): pl.pallas_call(kernel, name='combine', out_shape=(jax.ShapeDtypeStruct((T...]
    all_to_all x1 -> x0, blocking collectives: 55.9 us -> none  [sent_to_all(): return lax.all_to_all(copies, axis, split_axis=0, concat_axis=0, tiled=True)]
    all_to_all x1 -> x0, waiting for transfers between devices: 30.6 us -> none  [on_device(): lax.all_to_all(grouped, 'expert', split_axis=1, concat_axis=0, tiled=True)]
    all_to_all x1 -> x0, starting transfers between devices: 23.5 us -> none  [on_device(): lax.all_to_all(grouped, 'expert', split_axis=1, concat_axis=0, tiled=True)]
    gather x6 -> x0, local copies, waits for them, and re-layouts: 13 us -> none  [the longest x5 7.39 us: on_device(): slot_index = jnp.take_along_axis(before, expert_ids, axis=1)]
    dot_general x3 -> x0, matrix products: 9.08 us -> none  [the longest x1 6.49 us: on_device(): jnp.einsum('xsf,xfd->xsd', hidden, down_weight, preferred_element_type=jn...]
    unnamed x15 -> x5, local copies, waits for them, and re-layouts: 0.39 us -> 8.56 us
    pallas_call x0 -> x2, local copies, waits for them, and re-layouts: none -> 3.23 us  [on_device(): pl.pallas_call(kernel, name='combine', out_shape=(jax.ShapeDtypeStruct((T...]
  transfers between devices with their start and end apart: 1 -> 0, of which waited for: 1 -> 0; matrix products, arithmetic and copies ran while one was open for 6% -> 0% of each run, Pallas kernels for 0% -> 0%
where the time goes in v1:
time: 98.8 us; the launch traced here: 98 us
  Pallas kernels  82.1 us (83%)
  local copies, waits for them, and re-layouts  13.2 us (13%)
  other arithmetic  2.05 us (2%)
    pallas_call x1, Pallas kernels, on_device(): pl.pallas_call(kernel, name='combine', out_shape=(jax.ShapeDtypeStruct((T...  82.1 us
    unnamed x5, local copies, waits for them, and re-layouts  8.56 us
    pallas_call x2, local copies, waits for them, and re-layouts, on_device(): pl.pallas_call(kernel, name='combine', out_shape=(jax.ShapeDtypeStruct((T...  3.23 us

profile of v1, /device:TPU:1, one launch (start us, length us, event | category | flops | bytes accessed | tf_op | source)
XLA Modules:
  0.0 98.0 jit_solution(2043552381964132881)
XLA Ops:
  0.6 0.7 convert_element_type.3
  1.3 1.3 %maximum_bitcast_fusion.meta_ref = f32[16,128]{1,0:T(8,128)} fusion(f32[128,8]{0,1:T(8,128)} %param.10, f32[128,8]{0,1:T(8,128)S(1)} %convert_element_type.3), kind=kLoop, calls=%fused_computation.1 | loop fusion | flops 2048 | bytes 16384 | tf_op jit(solution)/shard_map/transpose | solution.py:398
  2.6 0.8 reshape.10
  3.4 0.1 pad_maximum_fusion
  3.5 0.6 reshape.11.gain_ref
  4.1 0.0 copy-start
  4.1 1.8 %copy.11.residual_ref = bf16[128,448]{1,0:T(8,128)(2,1)} copy(bf16[128,448]{0,1:T(8,128)(2,1)} %param.11) | data formatting | bytes 229376 | tf_op args[4]
  5.9 3.8 %copy.9 = bf16[1,2048,448]{2,1,0:T(8,128)(2,1)} copy(bf16[1,2048,448]{1,2,0:T(8,128)(2,1)} %param.8) | data formatting | bytes 3670016 | tf_op args[1]
  9.8 0.0 copy-done
  9.8 2.9 %copy.10.proj_ref = bf16[7168,132]{1,0:T(8,128)(2,1)} copy(bf16[7168,132]{0,1:T(8,128)(2,1)S(1)} %copy-done) | data formatting | bytes 3784704 | tf_op args[6]
  12.7 82.1 %combine.1 = (bf16[128,448]{1,0:T(8,128)(2,1)}, bf16[128,132]{1,0:T(8,128)(2,1)}) custom-call(bf16[1536,2048]{1,0:T(8,128)(2,1)} %bitcast.5, bf16[2048,448]{1,0:T(8,128)(2,1)} %bitcast.4, bf16[7168,132]{1,0:T(8,128)(2,1)} %copy.10.proj_ref, f32[16,128]{1,0:T(8,128)} %maximum_bitcast_fusion.meta_ref, bf16[128,448]{1,0:T(8,128)(2,1)} %copy.11.residual_ref, ...), custom_call_target="tpu_custom_call" | custom-call | tf_op jit(solution)/shard_map/combine/pallas_call | solution.py:405
  94.8 1.7 %copy.12 = bf16[128,448]{0,1:T(8,128)(2,1)} copy(bf16[128,448]{1,0:T(8,128)(2,1)} %get-tuple-element.2) | data formatting | bytes 229376 | tf_op jit(solution)/shard_map/combine/pallas_call | solution.py:405
  96.5 1.6 %copy.13 = bf16[128,132]{0,1:T(8,128)(2,1)} copy(bf16[128,132]{1,0:T(8,128)(2,1)} %get-tuple-element.3) | data formatting | bytes 67584 | tf_op jit(solution)/shard_map/combine/pallas_call | solution.py:405
  (1 shorter events, 0.0 us)
Async XLA Ops:
  4.1 5.6 %copy-start = (bf16[7168,132]{0,1:T(8,128)(2,1)S(1)}, bf16[7168,132]{0,1:T(8,128)(2,1)}, u32[]{:S(2)}) copy-start(bf16[7168,132]{0,1:T(8,128)(2,1)} %param.13) | copy-start | bytes 5677060
